TPU v7x, 128 devices: a whole 4x4x4 slice. The times are simulated.
128 devices in a mesh: grp: 32 (over y, x, core), own: 4 (over z).
Axes of the slice: x: 4, y: 4, z: 4, core: 2. Of those that a mesh axis runs over, the one named last changes fastest.
Arguments:
- background: bfloat16 [256, 1024, 512], P('grp', 'own'), may hold values from -6 to 6
- obs_ens: bfloat16 [256, 2048, 512], P('grp', 'own'), may hold values from -12 to 12
- innovation: bfloat16 [256, 2048], P('grp', 'own'), may hold values from -6 to 6
- obs_weight: bfloat16 [256, 2048], P('grp', 'own'), may hold values from 0.25 to 4
- obs_count: int32 [256, 4], P('grp', 'own'), may hold values from 128 to 512, as said below
- dest: int32 [256], replicated, may hold values from 0 to 31, as said below
Outputs:
- analysis: bfloat16 [256, 1024, 512], P('grp', 'own')
Inputs may be any that keep to these rules, and one draw needn't show every extreme that they name: `obs_count`: each entry counts the live leading slots of one owner's block of 512; later slots carry values that must be ignored. The largest entry of every draw equals 512. `dest`: every index of grp is named by exactly 8 groups, and no two groups of one index of grp name the same index.
All inputs are finite; a program needn't handle non-finite values.
Results may differ from a plain program's by a relative error of at most 0.012.
The roundings to bfloat16 on the way count: a program that leaves them out, or rounds other values in their place, can miss the bound.
Values may be sent and summed in bfloat16 or wider, within the bound.
A program may use at most 128 MiB of HBM per device.

v0:
```python
import jax
import jax.numpy as jnp
from jax import lax
from jax.sharding import PartitionSpec as P

NS_IT = 4


def newton_weights(gram, right_side):
    members = gram.shape[-1]
    eye_mat = jnp.eye(members, dtype=jnp.float32)
    matrix = gram + (members - 1.0) * eye_mat
    norm_scale = jnp.sqrt(jnp.sum(matrix * matrix, axis=(1, 2)))
    root_iter = (matrix / norm_scale[:, None, None]).astype(jnp.bfloat16)
    inverse = jnp.broadcast_to(eye_mat.astype(jnp.bfloat16), matrix.shape)
    for iteration in range(NS_IT):
        product = jnp.einsum("gij,gjk->gik", inverse, root_iter, preferred_element_type=jnp.float32)
        factor = (1.5 * eye_mat - 0.5 * product).astype(jnp.bfloat16)
        root_iter = jnp.einsum(
            "gij,gjk->gik", root_iter, factor, preferred_element_type=jnp.float32
        ).astype(jnp.bfloat16)
        inverse = jnp.einsum(
            "gij,gjk->gik", factor, inverse, preferred_element_type=jnp.float32
        ).astype(jnp.bfloat16)
    inverse_wide = inverse.astype(jnp.float32)
    half_way = jnp.einsum("gij,gj->gi", inverse_wide, right_side)
    mean_weight = jnp.einsum("gij,gj->gi", inverse_wide, half_way) / norm_scale[:, None]
    weights = (
        jnp.sqrt((members - 1.0) / norm_scale)[:, None, None] * inverse_wide
        + mean_weight[:, :, None]
    )
    return weights.astype(jnp.bfloat16)


def solve_weights(obs_pert, weight, source):
    weighted = (obs_pert.astype(jnp.float32) * weight.astype(jnp.float32)[:, :, None]).astype(
        jnp.bfloat16
    )
    gram_local = jnp.einsum("gpk,gpl->gkl", weighted, obs_pert, preferred_element_type=jnp.float32)
    right_local = jnp.einsum("gp,gpk->gk", source, obs_pert, preferred_element_type=jnp.float32)
    gram_part, right_part = (
        lax.psum_scatter(gram_local, "own", scatter_dimension=0, tiled=True),
        lax.psum_scatter(right_local, "own", scatter_dimension=0, tiled=True),
    )
    return lax.all_gather(newton_weights(gram_part, right_part), "own", axis=0, tiled=True)


def apply_weights(state_here, weights):
    state_mean = jnp.mean(state_here.astype(jnp.float32), axis=2, keepdims=True)
    state_pert = (state_here.astype(jnp.float32) - state_mean).astype(jnp.bfloat16)
    result = state_mean + jnp.einsum(
        "grk,gkl->grl", state_pert, weights, preferred_element_type=jnp.float32
    )
    return result.astype(jnp.bfloat16)


def pack_rows(array_in, send_index, send_live):
    picked = jnp.take(array_in, send_index, axis=0)
    keep_mask = send_live.reshape((-1,) + (1,) * (array_in.ndim - 1))
    return jnp.where(keep_mask, picked, jnp.zeros_like(picked))


def body(background, obs_ens, innovation, obs_weight, obs_count, dest):
    grp_size = lax.axis_size("grp")
    grp_index = lax.axis_index("grp")
    local_groups = background.shape[0]
    obs_rows = obs_ens.shape[1]
    obs_mean = jnp.mean(obs_ens.astype(jnp.float32), axis=2, keepdims=True)
    obs_pert = (obs_ens.astype(jnp.float32) - obs_mean).astype(jnp.bfloat16)
    position_in = lax.broadcasted_iota(jnp.int32, (local_groups, obs_rows), 1)
    live_rows = position_in < obs_count
    weight = jnp.where(live_rows, obs_weight, jnp.zeros_like(obs_weight))
    source = (weight.astype(jnp.float32) * innovation.astype(jnp.float32)).astype(jnp.bfloat16)
    group_total = dest.shape[0]
    group_ids = jnp.arange(group_total, dtype=jnp.int32)
    same_dest = dest[None, :] == dest[:, None]
    earlier = group_ids[None, :] < group_ids[:, None]
    arrival_rank = jnp.sum(jnp.where(same_dest & earlier, 1, 0), axis=1).astype(jnp.int32)
    my_dest = lax.dynamic_slice_in_dim(dest, grp_index * local_groups, local_groups)
    peer_ids = jnp.arange(grp_size, dtype=jnp.int32)
    local_ids = jnp.arange(local_groups, dtype=jnp.int32)
    peer_hits = my_dest[None, :] == peer_ids[:, None]
    send_index = jnp.sum(jnp.where(peer_hits, local_ids[None, :], 0), axis=1)
    send_live = jnp.any(peer_hits, axis=1)
    arriving = (dest[None, :] == grp_index) & (arrival_rank[None, :] == local_ids[:, None])
    arrive_group = jnp.sum(jnp.where(arriving, group_ids[None, :], 0), axis=1)
    arrive_source = arrive_group // local_groups
    weights = solve_weights(obs_pert, weight, source)
    result = apply_weights(background, weights)
    return jnp.take(
        lax.all_to_all(
            pack_rows(result, send_index, send_live), "grp", split_axis=0, concat_axis=0, tiled=True
        ),
        arrive_source,
        axis=0,
    )


def solution(mesh):
    return jax.shard_map(
        body,
        mesh=mesh,
        in_specs=(
            P("grp", "own", None),
            P("grp", "own", None),
            P("grp", "own"),
            P("grp", "own"),
            P("grp", "own"),
            P(),
        ),
        out_specs=P("grp", "own", None),
        check_vma=False,
    )
```

profile of v0, /device:TPU:0, one launch (start us, length us, event | category | flops | bytes accessed | tf_op | source)
XLA Modules:
  0.0 308.9 jit_solution(16136951597792057878)
XLA Ops:
  6.5 0.0 copy-start.6
  6.5 0.0 copy-start.3
  6.5 0.0 reduce-scatter.2.cloned.1.call-start
  6.5 0.0 copy-start
  6.5 3.0 convert_reduce_fusion
  9.5 0.0 copy-done.6
  9.5 0.0 copy-done.3
  9.5 0.1 fusion.16
  9.6 0.4 copy-done
  10.0 6.3 %fusion.1 = f32[8,512,512]{2,1,0:T(8,128)} fusion(f32[8,512]{1,0:T(8,128)S(1)} %fusion.16, bf16[8,512,512]{2,1,0:T(8,128)(2,1)S(1)} %copy-done, f32[8,512]{1,0:T(8,128)S(1)} %broadcast_multiply_fusion), kind=kOutput, calls=%fused_computation.7 | convolution fusion | flops 2166358016 | bytes 12615680 | tf_op jit(solution)/shard_map/gpk,gpl->gkl/dot_general | solution.py:39
  16.3 0.0 copy-start.5
  16.3 0.0 reduce-scatter.2.cloned.1.call-update
  16.3 0.0 all-gather.2.cloned.1.call-start
  16.4 0.6 copy-done.5
  17.0 0.1 fusion.17
  17.1 0.0 copy-start.7
  17.1 2.8 fusion.5
  19.9 0.0 copy-done.7
  19.9 0.6 dynamic-slice
  21.1 19.0 %all-reduce = bf16[8,512]{1,0:T(8,128)(2,1)S(1)} all-reduce(f32[8,512]{1,0:T(8,128)S(1)} %bitcast.53), channel_id=3, replica_groups=mesh['grp'=32,'own'=4] {'own'}, use_global_device_ids=true, to_apply=%region_8.9.clone | all-reduce | flops 4096 | bytes 24576
  40.1 0.1 fusion.10
  40.2 0.1 fusion.9
  40.4 59.6 %reduce-scatter.2.cloned.1.call-done = f32[2,512,512]{2,1,0:T(8,128)} async-done(((f32[8,512,512]{2,1,0:T(8,128)}), f32[2,512,512]{2,1,0:T(8,128)}) %reduce-scatter.2.cloned.1.call-update) | async-done | bytes 2097168 | tf_op jit(solution)/shard_map/reduce_scatter | solution.py:42
  100.0 0.0 copy-start.1
  100.0 2.1 multiply_reduce_fusion
  102.1 0.1 copy-done.1
  102.2 0.6 divide_convert_fusion
  102.8 0.7 subtract_convert_fusion.3
  103.5 0.7 convolution_convert_fusion.5
  104.2 0.7 convolution_convert_fusion.6
  105.0 0.7 subtract_convert_fusion.2
  105.7 0.7 convolution_convert_fusion.3
  106.4 0.7 convolution_convert_fusion.4
  107.1 0.7 subtract_convert_fusion.1
  107.9 0.0 copy-start.8
  107.9 1.0 copy-done.8
  108.9 1.7 convolution_convert_fusion.2
  110.5 3.8 %subtract_convert_fusion = bf16[2,512,512]{2,1,0:T(8,128)(2,1)} fusion(bf16[2,512,512]{2,1,0:T(8,128)(2,1)} %convolution_convert_fusion.2, bf16[2,512,512]{2,1,0:T(8,128)(2,1)S(1)} %convolution_convert_fusion.3, bf16[2,512,512]{2,1,0:T(8,128)(2,1)} %copy-done.8, f32[512,512]{1,0:T(8,128)S(1)} %fusion.9), kind=kOutput, calls=%fused_computation.15 | convolution fusion | flops 1075838976 | bytes 5242880 | tf_op jit(solution)/shard_map/gij,gjk->gik/dot_general | solution.py:17
  114.4 2.2 convolution_convert_fusion
  116.6 0.4 fusion.21
  117.0 0.0 copy-start.4
  117.0 0.0 copy-start.2
  117.0 0.4 fusion.19
  117.4 0.1 bitcast_divide_fusion
  117.5 1.3 add_convert_fusion.1
  118.8 0.0 all-gather.2.cloned.1.call-update
  118.8 0.0 copy-done.4
  118.8 0.1 dynamic_slice.3
  118.9 0.1 select_reduce_fusion.2
  119.0 0.1 fusion.23
  119.1 0.0 copy-done.2
  119.1 0.3 convert_reduce_fusion.1
  119.5 47.3 %all-gather.2.cloned.1.call-done = bf16[8,512,512]{2,1,0:T(8,128)(2,1)} async-done(((bf16[2,512,512]{2,1,0:T(8,128)(2,1)}), bf16[8,512,512]{2,1,0:T(8,128)(2,1)}) %all-gather.2.cloned.1.call-update) | async-done | bytes 4194320 | tf_op jit(solution)/shard_map/all_gather | solution.py:45
  166.8 4.1 %add_convert_fusion = bf16[8,256,512]{2,1,0:T(8,128)(2,1)S(1)} fusion(bf16[8,512,512]{2,1,0:T(8,128)(2,1)} %all-gather.2.cloned.1.call-done, bf16[8,256,512]{2,1,0:T(8,128)(2,1)} %param.6, f32[8,256]{1,0:T(8,128)S(1)} %broadcast_multiply_fusion.1), kind=kOutput, calls=%fused_computation.11 | convolution fusion | flops 1078984704 | bytes 8396800 | tf_op jit(solution)/shard_map/grk,gkl->grl/dot_general | solution.py:51
  170.9 4.8 %gather_fusion = bf16[32,256,512]{2,1,0:T(8,128)(2,1)} fusion(bf16[8,256,512]{2,1,0:T(8,128)(2,1)S(1)} %add_convert_fusion, s32[1024]{0:T(1024)S(1)} %pad_clamp_fusion.1), kind=kCustom, calls=%fused_computation | custom fusion | bytes 16777344 | tf_op jit(solution)/shard_map/jit(_take)/gather | solution.py:58
  175.8 7.6 %select_select_fusion = bf16[32,256,512]{2,1,0:T(8,128)(2,1)} fusion(bf16[32,256,512]{2,1,0:T(8,128)(2,1)} %gather_fusion, pred[32]{0:T(512)(128)(4,1)S(1)} %compare_and_fusion, pred[32]{0:T(512)(128)(4,1)S(1)} %fusion.23), kind=kLoop, calls=%fused_computation.5 | loop fusion | flops 8388608 | bytes 16777280 | tf_op jit(solution)/shard_map/jit(_where)/select_n | solution.py:60
  183.3 7.2 %all-to-all-start = ((bf16[32,256,512]{2,1,0:T(8,128)(2,1)}), bf16[32,256,512]{2,1,0:T(8,128)(2,1)}, u32[]{:S(2)}, u32[]{:S(2)}) async-start(bf16[32,256,512]{2,1,0:T(8,128)(2,1)} %select_select_fusion), calls=%async_computation.1 | async-start | bytes 16777216 | tf_op jit(solution)/shard_map/all_to_all | solution.py:91
  190.6 0.2 select_reduce_fusion
  190.8 0.1 select_reduce_fusion.1
  190.9 105.5 %all-to-all-done = bf16[32,256,512]{2,1,0:T(8,128)(2,1)} async-done(((bf16[32,256,512]{2,1,0:T(8,128)(2,1)}), bf16[32,256,512]{2,1,0:T(8,128)(2,1)}, u32[]{:S(2)}, u32[]{:S(2)}) %all-to-all-start) | async-done | bytes 8388640 | tf_op jit(solution)/shard_map/all_to_all | solution.py:91
  296.4 4.1 %gather_fusion.1 = bf16[8,256,512]{2,1,0:T(8,128)(2,1)S(1)} fusion(bf16[32,256,512]{2,1,0:T(8,128)(2,1)} %all-to-all-done, s32[1024]{0:T(1024)S(1)} %pad_clamp_fusion), kind=kCustom, calls=%fused_computation.1 | custom fusion | bytes 4194336 | tf_op jit(solution)/shard_map/jit(_take)/gather | solution.py:90
  300.5 1.6 broadcast_select_fusion
  (14 shorter events, 0.1 us)
Async XLA Ops:
  6.5 3.0 copy-start.6
  6.5 3.0 copy-start.3
  6.5 93.5 %reduce-scatter.2.cloned.1.call-start = ((), (), s32[]{:S(2)}) async-start(), calls=%async_computation.2 | async-start | bytes 10485760 | tf_op jit(solution)/shard_map/reduce_scatter | solution.py:42
  6.5 3.5 %copy-start = (bf16[8,512,512]{2,1,0:T(8,128)(2,1)S(1)}, bf16[8,512,512]{2,1,0:T(8,128)(2,1)}, u32[]{:S(2)}) copy-start(bf16[8,512,512]{2,1,0:T(8,128)(2,1)} %param.7) | copy-start | bytes 12582916
  16.3 0.7 copy-start.5
  16.3 150.4 %all-gather.2.cloned.1.call-start = ((), (), s32[]{:S(2)}) async-start(), calls=%async_computation.3 | async-start | bytes 5242880 | tf_op jit(solution)/shard_map/all_gather | solution.py:45
  17.1 2.8 copy-start.7
  100.0 2.2 copy-start.1
  107.9 1.0 copy-start.8
  117.0 1.8 copy-start.4
  117.0 2.1 copy-start.2
  183.3 113.1 %all-to-all-start = ((bf16[32,256,512]{2,1,0:T(8,128)(2,1)}), bf16[32,256,512]{2,1,0:T(8,128)(2,1)}, u32[]{:S(2)}, u32[]{:S(2)}) async-start(bf16[32,256,512]{2,1,0:T(8,128)(2,1)} %select_select_fusion), calls=%async_computation.1 | async-start | bytes 16777216 | tf_op jit(solution)/shard_map/all_to_all | solution.py:91
Sparse Core Ops, SparseCore 0:
  16.4 83.5 reduce-scatter.1
  118.9 47.8 all-gather.1
where the time goes:
time: 309 us
  waiting for transfers between devices  212 us (69%)
  matrix products  26.7 us (9%)
  blocking collectives  19 us (6%)
  other arithmetic  17.5 us (6%)
  between operations  14.3 us (5%)
  local copies, waits for them, and re-layouts  11.7 us (4%)
  starting transfers between devices  7.27 us (2%)
    all_to_all x1, waiting for transfers between devices, body(): lax.all_to_all(pack_rows(result, send_index, send_live), 'grp', split_axi...  105 us
    reduce_scatter x1, waiting for transfers between devices, solve_weights(): lax.psum_scatter(gram_local, 'own', scatter_dimension=0, tiled=True)  59.6 us
    all_gather x1, waiting for transfers between devices, solve_weights(): lax.all_gather(newton_weights(gram_part, right_part), 'own', axis=0, tile...  47.3 us
    unnamed x1, blocking collectives  19 us
    select_n x1, other arithmetic, pack_rows(): return jnp.where(keep_mask, picked, jnp.zeros_like(picked))  7.57 us
    all_to_all x1, starting transfers between devices, body(): lax.all_to_all(pack_rows(result, send_index, send_live), 'grp', split_axi...  7.23 us
    dot_general x1, matrix products, solve_weights(): jnp.einsum('gpk,gpl->gkl', weighted, obs_pert, preferred_element_type=jnp...  6.28 us
  transfers between devices with their start and end apart: 3, of which 3 were waited for; matrix products, arithmetic and copies ran while one was open for 2% of the time, Pallas kernels for 0%

commit v1 on v0

--- a/solution.py
+++ b/solution.py
@@ -1,9 +1,25 @@
+import functools
 import jax
 import jax.numpy as jnp
 from jax import lax
 from jax.sharding import PartitionSpec as P
 
 NS_IT = 4
+
+
+def _meet_zone(z_in, along_axis):
+    item_now = lax.axis_size(along_axis)
+    current_block = lax.all_to_all(
+        jnp.concatenate(item_now * [z_in], 0),
+        axis_name=along_axis,
+        concat_axis=0,
+        tiled=True,
+        split_axis=0,
+    )
+    return current_block
+
+
+state_vector = functools.partial(_meet_zone, along_axis="own")
 
 
 def newton_weights(gram, right_side):
@@ -42,7 +58,7 @@
         lax.psum_scatter(gram_local, "own", scatter_dimension=0, tiled=True),
         lax.psum_scatter(right_local, "own", scatter_dimension=0, tiled=True),
     )
-    return lax.all_gather(newton_weights(gram_part, right_part), "own", axis=0, tiled=True)
+    return state_vector(newton_weights(gram_part, right_part))
 
 
 def apply_weights(state_here, weights):

time: 309 us -> 317 us (1.026)
  starting transfers between devices: 7.27 us -> 12.4 us
    all_to_all x0 -> x1, waiting for transfers between devices: none -> 48.3 us  [_meet_zone(): lax.all_to_all(jnp.concatenate(item_now * [z_in], 0), axis_name=along_axi...]
    all_gather x1 -> x0, waiting for transfers between devices: 47.3 us -> none  [solve_weights(): lax.all_gather(newton_weights(gram_part, right_part), 'own', axis=0, tile...]
    all_to_all x0 -> x1, starting transfers between devices: none -> 5.17 us  [_meet_zone(): lax.all_to_all(jnp.concatenate(item_now * [z_in], 0), axis_name=along_axi...]
  transfers between devices with their start and end apart: 3 -> 3, of which waited for: 3 -> 3; matrix products, arithmetic and copies ran while one was open for 2% -> 1% of each run, Pallas kernels for 0% -> 0%
where the time goes in v1:
time: 317 us; the launch traced here: 316 us
  waiting for transfers between devices  213 us (67%)
  matrix products  26.7 us (8%)
  blocking collectives  18.9 us (6%)
  other arithmetic  18.8 us (6%)
  between operations  14.3 us (5%)
  starting transfers between devices  12.4 us (4%)
  local copies, waits for them, and re-layouts  11.7 us (4%)
    all_to_all x1, waiting for transfers between devices, body(): lax.all_to_all(pack_rows(result, send_index, send_live), 'grp', split_axi...  105 us
    reduce_scatter x1, waiting for transfers between devices, solve_weights(): lax.psum_scatter(gram_local, 'own', scatter_dimension=0, tiled=True)  59.7 us
    all_to_all x1, waiting for transfers between devices, _meet_zone(): lax.all_to_all(jnp.concatenate(item_now * [z_in], 0), axis_name=along_axi...  48.3 us
    unnamed x1, blocking collectives  18.9 us
    select_n x1, other arithmetic, pack_rows(): return jnp.where(keep_mask, picked, jnp.zeros_like(picked))  7.57 us
    all_to_all x1, starting transfers between devices, body(): lax.all_to_all(pack_rows(result, send_index, send_live), 'grp', split_axi...  7.23 us
  transfers between devices with their start and end apart: 3, of which 3 were waited for; matrix products, arithmetic and copies ran while one was open for 1% of the time, Pallas kernels for 0%

profile of v1, /device:TPU:0, one launch (start us, length us, event | category | flops | bytes accessed | tf_op | source)
XLA Modules:
  0.0 316.3 jit_solution(16771104277405262836)
XLA Ops:
  6.5 0.0 copy-start.6
  6.5 0.0 copy-start.3
  6.5 0.0 reduce-scatter.2.cloned.1.call-start
  6.5 0.0 copy-start
  6.5 3.0 convert_reduce_fusion
  9.5 0.0 copy-done.6
  9.5 0.0 copy-done.3
  9.5 0.1 fusion.16
  9.6 0.4 copy-done
  10.0 6.3 %fusion.1 = f32[8,512,512]{2,1,0:T(8,128)} fusion(f32[8,512]{1,0:T(8,128)S(1)} %fusion.16, bf16[8,512,512]{2,1,0:T(8,128)(2,1)S(1)} %copy-done, f32[8,512]{1,0:T(8,128)S(1)} %broadcast_multiply_fusion), kind=kOutput, calls=%fused_computation.7 | convolution fusion | flops 2166358016 | bytes 12615680 | tf_op jit(solution)/shard_map/gpk,gpl->gkl/dot_general | solution.py:55
  16.3 0.0 copy-start.5
  16.3 0.0 reduce-scatter.2.cloned.1.call-update
  16.3 0.0 copy-start.7
  16.3 0.7 copy-done.5
  17.0 0.1 fusion.17
  17.1 2.8 fusion.5
  19.8 0.0 copy-done.7
  19.8 0.6 dynamic-slice
  21.1 18.9 %all-reduce = bf16[8,512]{1,0:T(8,128)(2,1)S(1)} all-reduce(f32[8,512]{1,0:T(8,128)S(1)} %bitcast.53), channel_id=3, replica_groups=mesh['grp'=32,'own'=4] {'own'}, use_global_device_ids=true, to_apply=%region_8.9.clone | all-reduce | flops 4096 | bytes 24576
  40.1 0.1 fusion.10
  40.2 0.1 fusion.9
  40.3 59.7 %reduce-scatter.2.cloned.1.call-done = f32[2,512,512]{2,1,0:T(8,128)} async-done(((f32[8,512,512]{2,1,0:T(8,128)}), f32[2,512,512]{2,1,0:T(8,128)}) %reduce-scatter.2.cloned.1.call-update) | async-done | bytes 2097168 | tf_op jit(solution)/shard_map/reduce_scatter | solution.py:58
  100.0 0.0 copy-start.1
  100.0 2.1 multiply_reduce_fusion
  102.1 0.1 copy-done.1
  102.2 0.6 divide_convert_fusion
  102.8 0.7 subtract_convert_fusion.3
  103.5 0.7 convolution_convert_fusion.5
  104.2 0.7 convolution_convert_fusion.6
  105.0 0.7 subtract_convert_fusion.2
  105.7 0.7 convolution_convert_fusion.3
  106.4 0.7 convolution_convert_fusion.4
  107.1 0.7 subtract_convert_fusion.1
  107.9 0.0 copy-start.8
  107.9 1.0 copy-done.8
  108.9 1.7 convolution_convert_fusion.2
  110.5 3.8 %subtract_convert_fusion = bf16[2,512,512]{2,1,0:T(8,128)(2,1)} fusion(bf16[2,512,512]{2,1,0:T(8,128)(2,1)} %convolution_convert_fusion.2, bf16[2,512,512]{2,1,0:T(8,128)(2,1)S(1)} %convolution_convert_fusion.3, bf16[2,512,512]{2,1,0:T(8,128)(2,1)} %copy-done.8, f32[512,512]{1,0:T(8,128)S(1)} %fusion.9), kind=kOutput, calls=%fused_computation.16 | convolution fusion | flops 1075838976 | bytes 5242880 | tf_op jit(solution)/shard_map/gij,gjk->gik/dot_general | solution.py:33
  114.4 2.2 convolution_convert_fusion
  116.6 0.4 fusion.21
  117.0 0.4 fusion.19
  117.4 0.1 bitcast_divide_fusion
  117.5 0.3 add_convert_fusion.1
  117.8 2.3 pad_maximum_fusion
  120.1 0.0 copy-start.4
  120.1 0.0 copy-start.2
  120.1 5.2 %all-to-all-start = ((bf16[8,512,512]{2,1,0:T(8,128)(2,1)}), bf16[8,512,512]{2,1,0:T(8,128)(2,1)}, u32[]{:S(2)}, u32[]{:S(2)}) async-start(bf16[8,512,512]{2,1,0:T(8,128)(2,1)} %pad_maximum_fusion), calls=%async_computation.1 | async-start | bytes 8388608 | tf_op jit(solution)/shard_map/all_to_all | solution.py:12
  125.3 0.0 copy-done.4
  125.3 0.1 dynamic_slice.3
  125.3 0.1 select_reduce_fusion.2
  125.5 0.1 fusion.23
  125.5 0.0 copy-done.2
  125.5 0.3 convert_reduce_fusion.1
  125.9 48.3 %all-to-all-done = bf16[8,512,512]{2,1,0:T(8,128)(2,1)} async-done(((bf16[8,512,512]{2,1,0:T(8,128)(2,1)}), bf16[8,512,512]{2,1,0:T(8,128)(2,1)}, u32[]{:S(2)}, u32[]{:S(2)}) %all-to-all-start) | async-done | bytes 4194336 | tf_op jit(solution)/shard_map/all_to_all | solution.py:12
  174.2 4.1 %add_convert_fusion = bf16[8,256,512]{2,1,0:T(8,128)(2,1)S(1)} fusion(bf16[8,512,512]{2,1,0:T(8,128)(2,1)} %all-to-all-done, bf16[8,256,512]{2,1,0:T(8,128)(2,1)} %param.6, f32[8,256]{1,0:T(8,128)S(1)} %broadcast_multiply_fusion.1), kind=kOutput, calls=%fused_computation.12 | convolution fusion | flops 1078984704 | bytes 8396800 | tf_op jit(solution)/shard_map/grk,gkl->grl/dot_general | solution.py:67
  178.3 4.8 %gather_fusion = bf16[32,256,512]{2,1,0:T(8,128)(2,1)} fusion(bf16[8,256,512]{2,1,0:T(8,128)(2,1)S(1)} %add_convert_fusion, s32[1024]{0:T(1024)S(1)} %pad_clamp_fusion.1), kind=kCustom, calls=%fused_computation | custom fusion | bytes 16777344 | tf_op jit(solution)/shard_map/jit(_take)/gather | solution.py:74
  183.2 7.6 %select_select_fusion = bf16[32,256,512]{2,1,0:T(8,128)(2,1)} fusion(bf16[32,256,512]{2,1,0:T(8,128)(2,1)} %gather_fusion, pred[32]{0:T(512)(128)(4,1)S(1)} %compare_and_fusion, pred[32]{0:T(512)(128)(4,1)S(1)} %fusion.23), kind=kLoop, calls=%fused_computation.5 | loop fusion | flops 8388608 | bytes 16777280 | tf_op jit(solution)/shard_map/jit(_where)/select_n | solution.py:76
  190.7 7.2 %all-to-all-start.1 = ((bf16[32,256,512]{2,1,0:T(8,128)(2,1)}), bf16[32,256,512]{2,1,0:T(8,128)(2,1)}, u32[]{:S(2)}, u32[]{:S(2)}) async-start(bf16[32,256,512]{2,1,0:T(8,128)(2,1)} %select_select_fusion), calls=%async_computation.2 | async-start | bytes 16777216 | tf_op jit(solution)/shard_map/all_to_all | solution.py:107
  198.0 0.2 select_reduce_fusion
  198.2 0.1 select_reduce_fusion.1
  198.3 105.5 %all-to-all-done.1 = bf16[32,256,512]{2,1,0:T(8,128)(2,1)} async-done(((bf16[32,256,512]{2,1,0:T(8,128)(2,1)}), bf16[32,256,512]{2,1,0:T(8,128)(2,1)}, u32[]{:S(2)}, u32[]{:S(2)}) %all-to-all-start.1) | async-done | bytes 8388640 | tf_op jit(solution)/shard_map/all_to_all | solution.py:107
  303.8 4.1 %gather_fusion.1 = bf16[8,256,512]{2,1,0:T(8,128)(2,1)S(1)} fusion(bf16[32,256,512]{2,1,0:T(8,128)(2,1)} %all-to-all-done.1, s32[1024]{0:T(1024)S(1)} %pad_clamp_fusion), kind=kCustom, calls=%fused_computation.1 | custom fusion | bytes 4194336 | tf_op jit(solution)/shard_map/jit(_take)/gather | solution.py:106
  307.9 1.6 broadcast_select_fusion
  (14 shorter events, 0.1 us)
Async XLA Ops:
  6.5 3.0 copy-start.6
  6.5 3.0 copy-start.3
  6.5 93.5 %reduce-scatter.2.cloned.1.call-start = ((), (), s32[]{:S(2)}) async-start(), calls=%async_computation.3 | async-start | bytes 10485760 | tf_op jit(solution)/shard_map/reduce_scatter | solution.py:58
  6.5 3.5 %copy-start = (bf16[8,512,512]{2,1,0:T(8,128)(2,1)S(1)}, bf16[8,512,512]{2,1,0:T(8,128)(2,1)}, u32[]{:S(2)}) copy-start(bf16[8,512,512]{2,1,0:T(8,128)(2,1)} %param.7) | copy-start | bytes 12582916
  16.3 0.7 copy-start.5
  16.3 3.5 %copy-start.7 = (u32[128]{0:T(128)S(1)}, u32[128]{0:T(128)}, u32[]{:S(2)}) copy-start(u32[128]{0:T(128)} %constant.82) | copy-start | bytes 1540
  100.0 2.2 copy-start.1
  107.9 1.0 copy-start.8
  120.1 5.2 %copy-start.4 = (s32[256]{0:T(256)S(1)}, s32[256]{0:T(256)}, u32[]{:S(2)}) copy-start(s32[256]{0:T(256)} %param.11) | copy-start | bytes 3076
  120.1 5.5 %copy-start.2 = (bf16[8,256,512]{2,1,0:T(8,128)(2,1)S(1)}, bf16[8,256,512]{2,1,0:T(8,128)(2,1)}, u32[]{:S(2)}) copy-start(bf16[8,256,512]{2,1,0:T(8,128)(2,1)} %param.6) | copy-start | bytes 6291460
  120.1 54.1 %all-to-all-start = ((bf16[8,512,512]{2,1,0:T(8,128)(2,1)}), bf16[8,512,512]{2,1,0:T(8,128)(2,1)}, u32[]{:S(2)}, u32[]{:S(2)}) async-start(bf16[8,512,512]{2,1,0:T(8,128)(2,1)} %pad_maximum_fusion), calls=%async_computation.1 | async-start | bytes 8388608 | tf_op jit(solution)/shard_map/all_to_all | solution.py:12
  190.7 113.1 %all-to-all-start.1 = ((bf16[32,256,512]{2,1,0:T(8,128)(2,1)}), bf16[32,256,512]{2,1,0:T(8,128)(2,1)}, u32[]{:S(2)}, u32[]{:S(2)}) async-start(bf16[32,256,512]{2,1,0:T(8,128)(2,1)} %select_select_fusion), calls=%async_computation.2 | async-start | bytes 16777216 | tf_op jit(solution)/shard_map/all_to_all | solution.py:107
Sparse Core Ops, SparseCore 0:
  16.4 83.5 reduce-scatter.1
